TPU v7x, 32 devices: a whole 2x2x4 slice. The times are simulated.
32 devices in a mesh: layer: 8 (over y, x, core), tile: 4 (over z).
Axes of the slice: x: 2, y: 2, z: 4, core: 2. Of those that a mesh axis runs over, the one named last changes fastest.
Arguments:
- incident: bfloat16 [4096, 128], P('tile'), may hold values from -6 to 6
- interface: bfloat16 [16, 4096, 4096], P('layer', 'tile'), may hold values from -0.09375 to 0.09375
- eigvec: bfloat16 [16, 4096, 4096], P('layer', 'tile'), may hold values from -0.09375 to 0.09375
- angle: float32 [16, 4096], P('layer'), may hold values from -3.140625 to 3.140625
- decay: float32 [16, 4096], P('layer'), may hold values from 0.002 to 0.15
Outputs:
- fields: bfloat16 [16, 4096, 512], P('layer', 'tile')
- leaving: float32 [16, 4096, 128], P('layer', 'tile')
All inputs are finite; a program needn't handle non-finite values.
Results may differ from a plain program's by a relative error of at most 0.035.
Values sent between devices are 32-bit elements; how exact they have to be, the bound alone decides.
A program may use at most 128 MiB of HBM per device.

v0:
```python
import jax
import jax.numpy as jnp
from jax import lax
from jax.sharding import PartitionSpec as P

DEPTHS = 4


def shifted(x, axis, by):
    peers = lax.axis_size(axis)
    pairs = [(i, i + by) for i in range(peers) if 0 <= i + by < peers]
    return lax.ppermute(x, axis, pairs)


def rotate(block, angle_row, decay_row, frac):
    half = block.shape[1] // 2
    real_part = block[:, :half]
    imag_part = block[:, half:]
    scale = jnp.exp(-frac * decay_row)
    cosine = (scale * jnp.cos(frac * angle_row))[:, None]
    sine = (scale * jnp.sin(frac * angle_row))[:, None]
    return jnp.concatenate(
        [cosine * real_part - sine * imag_part, sine * real_part + cosine * imag_part], axis=1
    )


def advance(current, interface, angle, decay):
    fulls = []
    leaves = []
    for layer_num in range(interface.shape[0]):
        full = lax.all_gather(current, "tile", axis=0, tiled=True)
        fulls.append(full)
        phased = rotate(full, angle[layer_num], decay[layer_num], 1.0).astype(jnp.bfloat16)
        current = jnp.dot(interface[layer_num], phased, preferred_element_type=jnp.float32)
        leaves.append(current)
    return (jnp.stack(fulls), jnp.stack(leaves))


def pick_block(values, block_num, block_width, half):
    real_part = lax.dynamic_slice_in_dim(
        values, block_num * block_width, block_width, values.ndim - 1
    )
    imag_part = lax.dynamic_slice_in_dim(
        values, half + block_num * block_width, block_width, values.ndim - 1
    )
    return jnp.concatenate([real_part, imag_part], axis=values.ndim - 1)


def put_block(values, piece, block_num, block_width, half):
    last = values.ndim - 1
    real_piece = lax.slice_in_dim(piece, 0, block_width, axis=last)
    imag_piece = lax.slice_in_dim(piece, block_width, 2 * block_width, axis=last)
    values = lax.dynamic_update_slice_in_dim(values, real_piece, block_num * block_width, last)
    return lax.dynamic_update_slice_in_dim(values, imag_piece, half + block_num * block_width, last)


def on_device(incident, interface, eigvec, angle, decay):
    groups = lax.axis_size("layer")
    member = lax.axis_index("layer")
    layers_here = interface.shape[0]
    shard_rows = interface.shape[1]
    orders = interface.shape[2]
    width = incident.shape[1]
    half = width // 2
    start_amps = incident.astype(jnp.float32)
    store_full = jnp.zeros((layers_here, orders, width), jnp.float32)
    store_leave = jnp.zeros((layers_here, shard_rows, width), jnp.float32)
    block_count = 4
    block_width = half // block_count
    inbox = jnp.zeros((shard_rows, 2 * block_width), jnp.float32)

    def step_blocks(step, carry):
        inbox, store_full, store_leave = carry
        block_num = step - member
        valid = (block_num >= 0) & (block_num < block_count)
        clipped = jnp.clip(block_num, 0, block_count - 1)
        source = jnp.where(member == 0, pick_block(start_amps, clipped, block_width, half), inbox)
        fulls, leaves = advance(source, interface, angle, decay)
        store_full = jnp.where(
            valid, put_block(store_full, fulls, clipped, block_width, half), store_full
        )
        store_leave = jnp.where(
            valid, put_block(store_leave, leaves, clipped, block_width, half), store_leave
        )
        inbox = shifted(leaves[layers_here - 1], "layer", 1)
        return (inbox, store_full, store_leave)

    inbox, store_full, store_leave = lax.fori_loop(
        0, groups + block_count - 1, step_blocks, (inbox, store_full, store_leave)
    )
    fields = []
    for layer_num in range(layers_here):
        depth = jnp.concatenate(
            [
                rotate(
                    store_full[layer_num], angle[layer_num], decay[layer_num], step / DEPTHS
                ).astype(jnp.bfloat16)
                for step in range(DEPTHS)
            ],
            axis=1,
        )
        fields.append(
            jnp.dot(eigvec[layer_num], depth, preferred_element_type=jnp.float32).astype(
                jnp.bfloat16
            )
        )
    return (jnp.stack(fields), store_leave)


def solution(mesh):
    in_specs = (
        P("tile", None),
        P("layer", "tile", None),
        P("layer", "tile", None),
        P("layer", None),
        P("layer", None),
    )
    out_specs = (P("layer", "tile", None), P("layer", "tile", None))
    return jax.shard_map(
        on_device, mesh=mesh, in_specs=in_specs, out_specs=out_specs, check_vma=False
    )
```

profile of v0, /device:TPU:1, one launch (start us, length us, event | category | flops | bytes accessed | tf_op | source)
XLA Modules:
  0.0 704.2 jit_solution(1159093125117101727)
XLA Ops:
  11.3 665.6 %while.20 = (s32[]{:T(128)}, f32[1024,32]{0,1:T(8,128)S(1)}, f32[2,4096,128]{1,2,0:T(8,128)}, f32[2,1024,128]{1,2,0:T(8,128)S(1)}, f32[2,4096]{1,0:T(2,128)}, /*...) while((s32[]{:T(128)}, f32[1024,32]{0,1:T(8,128)S(1)}, ...), condition=%wide.region_1.2_spmd.clone, body=%wide.region_0.1_spmd.clone.sunk | while | flops 543318016 | bytes 56263120 | solution.py:88
  12.3 15.3 %all_gather.24 = f32[4096,32]{0,1:T(8,128)S(1)} all-gather(f32[1024,32]{0,1:T(8,128)S(1)} %maximum_select_fusion.2), channel_id=1, replica_groups=mesh['layer'=8,'tile'=4] {'tile'}, dimensions={0}, use_global_device_ids=true | all-gather | bytes 655360 | tf_op jit(solution)/shard_map/while/body/eval_jaxpr/all_gather | solution.py:31
  28.4 6.0 fusion.75
  34.4 11.9 %all_gather.25 = f32[4096,32]{0,1:T(8,128)S(1)} all-gather(f32[1024,32]{0,1:T(8,128)S(1)} %bitcast.104), channel_id=1, replica_groups=mesh['layer'=8,'tile'=4] {'tile'}, dimensions={0}, use_global_device_ids=true | all-gather | bytes 655360 | tf_op jit(solution)/shard_map/while/body/eval_jaxpr/all_gather | solution.py:31
  47.1 6.0 fusion.77
  53.0 9.5 %collective-permute-start = (f32[1024,32]{0,1:T(8,128)S(1)}, f32[1024,32]{0,1:T(8,128)S(1)}, u32[]{:S(2)}, u32[]{:S(2)}) collective-permute-start(f32[1024,32]{0,1:T(8,128)S(1)} %bitcast.107), channel_id=1, source_target_pairs={{0,4},{4,8},{8,12},{12,16},{16,20},{20,24},{24,28},{1,5},{5,9},{9,... | collective-permute-start | bytes 393224 | tf_op jit(solution)/shard_map/while/body/eval_jaxpr/ppermute | solution.py:12
  71.0 13.6 %all_gather.24 = f32[4096,32]{0,1:T(8,128)S(1)} all-gather(f32[1024,32]{0,1:T(8,128)S(1)} %maximum_select_fusion.2), channel_id=1, replica_groups=mesh['layer'=8,'tile'=4] {'tile'}, dimensions={0}, use_global_device_ids=true | all-gather | bytes 655360 | tf_op jit(solution)/shard_map/while/body/eval_jaxpr/all_gather | solution.py:31
  85.3 6.0 fusion.75
  91.3 11.9 %all_gather.25 = f32[4096,32]{0,1:T(8,128)S(1)} all-gather(f32[1024,32]{0,1:T(8,128)S(1)} %bitcast.104), channel_id=1, replica_groups=mesh['layer'=8,'tile'=4] {'tile'}, dimensions={0}, use_global_device_ids=true | all-gather | bytes 655360 | tf_op jit(solution)/shard_map/while/body/eval_jaxpr/all_gather | solution.py:31
  104.0 6.0 fusion.77
  109.9 8.0 %collective-permute-start = (f32[1024,32]{0,1:T(8,128)S(1)}, f32[1024,32]{0,1:T(8,128)S(1)}, u32[]{:S(2)}, u32[]{:S(2)}) collective-permute-start(f32[1024,32]{0,1:T(8,128)S(1)} %bitcast.107), channel_id=1, source_target_pairs={{0,4},{4,8},{8,12},{12,16},{16,20},{20,24},{24,28},{1,5},{5,9},{9,... | collective-permute-start | bytes 393224 | tf_op jit(solution)/shard_map/while/body/eval_jaxpr/ppermute | solution.py:12
  124.4 6.3 broadcast_select_fusion.9
  132.1 14.9 %all_gather.24 = f32[4096,32]{0,1:T(8,128)S(1)} all-gather(f32[1024,32]{0,1:T(8,128)S(1)} %maximum_select_fusion.2), channel_id=1, replica_groups=mesh['layer'=8,'tile'=4] {'tile'}, dimensions={0}, use_global_device_ids=true | all-gather | bytes 655360 | tf_op jit(solution)/shard_map/while/body/eval_jaxpr/all_gather | solution.py:31
  153.7 14.3 %all_gather.25 = f32[4096,32]{0,1:T(8,128)S(1)} all-gather(f32[1024,32]{0,1:T(8,128)S(1)} %bitcast.104), channel_id=1, replica_groups=mesh['layer'=8,'tile'=4] {'tile'}, dimensions={0}, use_global_device_ids=true | all-gather | bytes 655360 | tf_op jit(solution)/shard_map/while/body/eval_jaxpr/all_gather | solution.py:31
  168.8 6.0 fusion.77
  185.5 6.3 broadcast_select_fusion.9
  193.1 15.5 %all_gather.24 = f32[4096,32]{0,1:T(8,128)S(1)} all-gather(f32[1024,32]{0,1:T(8,128)S(1)} %maximum_select_fusion.2), channel_id=1, replica_groups=mesh['layer'=8,'tile'=4] {'tile'}, dimensions={0}, use_global_device_ids=true | all-gather | bytes 655360 | tf_op jit(solution)/shard_map/while/body/eval_jaxpr/all_gather | solution.py:31
  215.4 13.9 %all_gather.25 = f32[4096,32]{0,1:T(8,128)S(1)} all-gather(f32[1024,32]{0,1:T(8,128)S(1)} %bitcast.104), channel_id=1, replica_groups=mesh['layer'=8,'tile'=4] {'tile'}, dimensions={0}, use_global_device_ids=true | all-gather | bytes 655360 | tf_op jit(solution)/shard_map/while/body/eval_jaxpr/all_gather | solution.py:31
  230.1 6.0 fusion.77
  247.6 6.3 broadcast_select_fusion.9
  255.2 14.3 %all_gather.24 = f32[4096,32]{0,1:T(8,128)S(1)} all-gather(f32[1024,32]{0,1:T(8,128)S(1)} %maximum_select_fusion.2), channel_id=1, replica_groups=mesh['layer'=8,'tile'=4] {'tile'}, dimensions={0}, use_global_device_ids=true | all-gather | bytes 655360 | tf_op jit(solution)/shard_map/while/body/eval_jaxpr/all_gather | solution.py:31
  270.3 6.0 fusion.75
  276.2 13.6 %all_gather.25 = f32[4096,32]{0,1:T(8,128)S(1)} all-gather(f32[1024,32]{0,1:T(8,128)S(1)} %bitcast.104), channel_id=1, replica_groups=mesh['layer'=8,'tile'=4] {'tile'}, dimensions={0}, use_global_device_ids=true | all-gather | bytes 655360 | tf_op jit(solution)/shard_map/while/body/eval_jaxpr/all_gather | solution.py:31
  290.7 6.0 fusion.77
  308.7 6.3 broadcast_select_fusion.9
  316.4 14.3 %all_gather.24 = f32[4096,32]{0,1:T(8,128)S(1)} all-gather(f32[1024,32]{0,1:T(8,128)S(1)} %maximum_select_fusion.2), channel_id=1, replica_groups=mesh['layer'=8,'tile'=4] {'tile'}, dimensions={0}, use_global_device_ids=true | all-gather | bytes 655360 | tf_op jit(solution)/shard_map/while/body/eval_jaxpr/all_gather | solution.py:31
  337.4 13.9 %all_gather.25 = f32[4096,32]{0,1:T(8,128)S(1)} all-gather(f32[1024,32]{0,1:T(8,128)S(1)} %bitcast.104), channel_id=1, replica_groups=mesh['layer'=8,'tile'=4] {'tile'}, dimensions={0}, use_global_device_ids=true | all-gather | bytes 655360 | tf_op jit(solution)/shard_map/while/body/eval_jaxpr/all_gather | solution.py:31
  352.1 6.0 fusion.77
  376.7 13.5 %all_gather.24 = f32[4096,32]{0,1:T(8,128)S(1)} all-gather(f32[1024,32]{0,1:T(8,128)S(1)} %maximum_select_fusion.2), channel_id=1, replica_groups=mesh['layer'=8,'tile'=4] {'tile'}, dimensions={0}, use_global_device_ids=true | all-gather | bytes 655360 | tf_op jit(solution)/shard_map/while/body/eval_jaxpr/all_gather | solution.py:31
  391.0 6.0 fusion.75
  397.0 13.6 %all_gather.25 = f32[4096,32]{0,1:T(8,128)S(1)} all-gather(f32[1024,32]{0,1:T(8,128)S(1)} %bitcast.104), channel_id=1, replica_groups=mesh['layer'=8,'tile'=4] {'tile'}, dimensions={0}, use_global_device_ids=true | all-gather | bytes 655360 | tf_op jit(solution)/shard_map/while/body/eval_jaxpr/all_gather | solution.py:31
  417.3 7.9 %collective-permute-start = (f32[1024,32]{0,1:T(8,128)S(1)}, f32[1024,32]{0,1:T(8,128)S(1)}, u32[]{:S(2)}, u32[]{:S(2)}) collective-permute-start(f32[1024,32]{0,1:T(8,128)S(1)} %bitcast.107), channel_id=1, source_target_pairs={{0,4},{4,8},{8,12},{12,16},{16,20},{20,24},{24,28},{1,5},{5,9},{9,... | collective-permute-start | bytes 393224 | tf_op jit(solution)/shard_map/while/body/eval_jaxpr/ppermute | solution.py:12
  438.2 12.0 %all_gather.24 = f32[4096,32]{0,1:T(8,128)S(1)} all-gather(f32[1024,32]{0,1:T(8,128)S(1)} %maximum_select_fusion.2), channel_id=1, replica_groups=mesh['layer'=8,'tile'=4] {'tile'}, dimensions={0}, use_global_device_ids=true | all-gather | bytes 655360 | tf_op jit(solution)/shard_map/while/body/eval_jaxpr/all_gather | solution.py:31
  456.9 14.2 %all_gather.25 = f32[4096,32]{0,1:T(8,128)S(1)} all-gather(f32[1024,32]{0,1:T(8,128)S(1)} %bitcast.104), channel_id=1, replica_groups=mesh['layer'=8,'tile'=4] {'tile'}, dimensions={0}, use_global_device_ids=true | all-gather | bytes 655360 | tf_op jit(solution)/shard_map/while/body/eval_jaxpr/all_gather | solution.py:31
  472.0 6.0 fusion.77
  477.9 7.3 %collective-permute-start = (f32[1024,32]{0,1:T(8,128)S(1)}, f32[1024,32]{0,1:T(8,128)S(1)}, u32[]{:S(2)}, u32[]{:S(2)}) collective-permute-start(f32[1024,32]{0,1:T(8,128)S(1)} %bitcast.107), channel_id=1, source_target_pairs={{0,4},{4,8},{8,12},{12,16},{16,20},{20,24},{24,28},{1,5},{5,9},{9,... | collective-permute-start | bytes 393224 | tf_op jit(solution)/shard_map/while/body/eval_jaxpr/ppermute | solution.py:12
  498.2 12.1 %all_gather.24 = f32[4096,32]{0,1:T(8,128)S(1)} all-gather(f32[1024,32]{0,1:T(8,128)S(1)} %maximum_select_fusion.2), channel_id=1, replica_groups=mesh['layer'=8,'tile'=4] {'tile'}, dimensions={0}, use_global_device_ids=true | all-gather | bytes 655360 | tf_op jit(solution)/shard_map/while/body/eval_jaxpr/all_gather | solution.py:31
  517.0 14.0 %all_gather.25 = f32[4096,32]{0,1:T(8,128)S(1)} all-gather(f32[1024,32]{0,1:T(8,128)S(1)} %bitcast.104), channel_id=1, replica_groups=mesh['layer'=8,'tile'=4] {'tile'}, dimensions={0}, use_global_device_ids=true | all-gather | bytes 655360 | tf_op jit(solution)/shard_map/while/body/eval_jaxpr/all_gather | solution.py:31
  537.8 7.2 %collective-permute-start = (f32[1024,32]{0,1:T(8,128)S(1)}, f32[1024,32]{0,1:T(8,128)S(1)}, u32[]{:S(2)}, u32[]{:S(2)}) collective-permute-start(f32[1024,32]{0,1:T(8,128)S(1)} %bitcast.107), channel_id=1, source_target_pairs={{0,4},{4,8},{8,12},{12,16},{16,20},{20,24},{24,28},{1,5},{5,9},{9,... | collective-permute-start | bytes 393224 | tf_op jit(solution)/shard_map/while/body/eval_jaxpr/ppermute | solution.py:12
  558.0 12.3 %all_gather.24 = f32[4096,32]{0,1:T(8,128)S(1)} all-gather(f32[1024,32]{0,1:T(8,128)S(1)} %maximum_select_fusion.2), channel_id=1, replica_groups=mesh['layer'=8,'tile'=4] {'tile'}, dimensions={0}, use_global_device_ids=true | all-gather | bytes 655360 | tf_op jit(solution)/shard_map/while/body/eval_jaxpr/all_gather | solution.py:31
  577.1 13.9 %all_gather.25 = f32[4096,32]{0,1:T(8,128)S(1)} all-gather(f32[1024,32]{0,1:T(8,128)S(1)} %bitcast.104), channel_id=1, replica_groups=mesh['layer'=8,'tile'=4] {'tile'}, dimensions={0}, use_global_device_ids=true | all-gather | bytes 655360 | tf_op jit(solution)/shard_map/while/body/eval_jaxpr/all_gather | solution.py:31
  591.8 6.0 fusion.77
  597.8 7.2 %collective-permute-start = (f32[1024,32]{0,1:T(8,128)S(1)}, f32[1024,32]{0,1:T(8,128)S(1)}, u32[]{:S(2)}, u32[]{:S(2)}) collective-permute-start(f32[1024,32]{0,1:T(8,128)S(1)} %bitcast.107), channel_id=1, source_target_pairs={{0,4},{4,8},{8,12},{12,16},{16,20},{20,24},{24,28},{1,5},{5,9},{9,... | collective-permute-start | bytes 393224 | tf_op jit(solution)/shard_map/while/body/eval_jaxpr/ppermute | solution.py:12
  617.9 12.3 %all_gather.24 = f32[4096,32]{0,1:T(8,128)S(1)} all-gather(f32[1024,32]{0,1:T(8,128)S(1)} %maximum_select_fusion.2), channel_id=1, replica_groups=mesh['layer'=8,'tile'=4] {'tile'}, dimensions={0}, use_global_device_ids=true | all-gather | bytes 655360 | tf_op jit(solution)/shard_map/while/body/eval_jaxpr/all_gather | solution.py:31
  636.9 14.3 %all_gather.25 = f32[4096,32]{0,1:T(8,128)S(1)} all-gather(f32[1024,32]{0,1:T(8,128)S(1)} %bitcast.104), channel_id=1, replica_groups=mesh['layer'=8,'tile'=4] {'tile'}, dimensions={0}, use_global_device_ids=true | all-gather | bytes 655360 | tf_op jit(solution)/shard_map/while/body/eval_jaxpr/all_gather | solution.py:31
  658.0 6.9 collective-permute-start
  685.7 7.3 %fusion.35 = bf16[1,1024,512]{1,2,0:T(8,128)(2,1)S(1)} fusion(bf16[4096,512]{0,1:T(8,128)(2,1)S(1)} %fusion.45, bf16[2,1024,4096]{2,1,0:T(8,128)(2,1)} %param.9), kind=kOutput, calls=%fused_computation.51 | convolution fusion | flops 4295491584 | bytes 13631488 | tf_op jit(solution)/shard_map/dot_general | solution.py:103
  694.4 7.1 %fusion.32 = bf16[1,1024,512]{1,2,0:T(8,128)(2,1)S(1)} fusion(bf16[4096,512]{0,1:T(8,128)(2,1)S(1)} %fusion.53, bf16[2,1024,4096]{2,1,0:T(8,128)(2,1)} %param.9), kind=kOutput, calls=%fused_computation.50 | convolution fusion | flops 4295491584 | bytes 13631488 | tf_op jit(solution)/shard_map/dot_general | solution.py:103
  (290 shorter events, 237.3 us)
Async XLA Ops:
  11.3 1.0 copy-start.1
  53.0 16.9 %collective-permute-start = (f32[1024,32]{0,1:T(8,128)S(1)}, f32[1024,32]{0,1:T(8,128)S(1)}, u32[]{:S(2)}, u32[]{:S(2)}) collective-permute-start(f32[1024,32]{0,1:T(8,128)S(1)} %bitcast.107), channel_id=1, source_target_pairs={{0,4},{4,8},{8,12},{12,16},{16,20},{20,24},{24,28},{1,5},{5,9},{9,... | collective-permute-start | bytes 393224 | tf_op jit(solution)/shard_map/while/body/eval_jaxpr/ppermute | solution.py:12
  66.8 3.1 copy-start.2
  69.9 1.0 copy-start.1
  109.9 21.1 %collective-permute-start = (f32[1024,32]{0,1:T(8,128)S(1)}, f32[1024,32]{0,1:T(8,128)S(1)}, u32[]{:S(2)}, u32[]{:S(2)}) collective-permute-start(f32[1024,32]{0,1:T(8,128)S(1)} %bitcast.107), channel_id=1, source_target_pairs={{0,4},{4,8},{8,12},{12,16},{16,20},{20,24},{24,28},{1,5},{5,9},{9,... | collective-permute-start | bytes 393224 | tf_op jit(solution)/shard_map/while/body/eval_jaxpr/ppermute | solution.py:12
  124.4 6.6 copy-start.2
  131.1 1.0 copy-start.1
  174.8 17.3 %collective-permute-start = (f32[1024,32]{0,1:T(8,128)S(1)}, f32[1024,32]{0,1:T(8,128)S(1)}, u32[]{:S(2)}, u32[]{:S(2)}) collective-permute-start(f32[1024,32]{0,1:T(8,128)S(1)} %bitcast.107), channel_id=1, source_target_pairs={{0,4},{4,8},{8,12},{12,16},{16,20},{20,24},{24,28},{1,5},{5,9},{9,... | collective-permute-start | bytes 393224 | tf_op jit(solution)/shard_map/while/body/eval_jaxpr/ppermute | solution.py:12
  185.5 6.6 copy-start.2
  192.1 1.0 copy-start.1
  236.1 18.1 %collective-permute-start = (f32[1024,32]{0,1:T(8,128)S(1)}, f32[1024,32]{0,1:T(8,128)S(1)}, u32[]{:S(2)}, u32[]{:S(2)}) collective-permute-start(f32[1024,32]{0,1:T(8,128)S(1)} %bitcast.107), channel_id=1, source_target_pairs={{0,4},{4,8},{8,12},{12,16},{16,20},{20,24},{24,28},{1,5},{5,9},{9,... | collective-permute-start | bytes 393224 | tf_op jit(solution)/shard_map/while/body/eval_jaxpr/ppermute | solution.py:12
  247.6 6.6 copy-start.2
  254.2 1.0 copy-start.1
  296.6 18.7 %collective-permute-start = (f32[1024,32]{0,1:T(8,128)S(1)}, f32[1024,32]{0,1:T(8,128)S(1)}, u32[]{:S(2)}, u32[]{:S(2)}) collective-permute-start(f32[1024,32]{0,1:T(8,128)S(1)} %bitcast.107), channel_id=1, source_target_pairs={{0,4},{4,8},{8,12},{12,16},{16,20},{20,24},{24,28},{1,5},{5,9},{9,... | collective-permute-start | bytes 393224 | tf_op jit(solution)/shard_map/while/body/eval_jaxpr/ppermute | solution.py:12
  308.7 6.6 copy-start.2
  315.4 1.0 copy-start.1
  358.0 17.6 %collective-permute-start = (f32[1024,32]{0,1:T(8,128)S(1)}, f32[1024,32]{0,1:T(8,128)S(1)}, u32[]{:S(2)}, u32[]{:S(2)}) collective-permute-start(f32[1024,32]{0,1:T(8,128)S(1)} %bitcast.107), channel_id=1, source_target_pairs={{0,4},{4,8},{8,12},{12,16},{16,20},{20,24},{24,28},{1,5},{5,9},{9,... | collective-permute-start | bytes 393224 | tf_op jit(solution)/shard_map/while/body/eval_jaxpr/ppermute | solution.py:12
  370.3 5.3 copy-start.2
  375.7 1.0 copy-start.1
  417.3 19.8 %collective-permute-start = (f32[1024,32]{0,1:T(8,128)S(1)}, f32[1024,32]{0,1:T(8,128)S(1)}, u32[]{:S(2)}, u32[]{:S(2)}) collective-permute-start(f32[1024,32]{0,1:T(8,128)S(1)} %bitcast.107), channel_id=1, source_target_pairs={{0,4},{4,8},{8,12},{12,16},{16,20},{20,24},{24,28},{1,5},{5,9},{9,... | collective-permute-start | bytes 393224 | tf_op jit(solution)/shard_map/while/body/eval_jaxpr/ppermute | solution.py:12
  431.8 5.3 copy-start.2
  437.1 1.0 copy-start.1
  477.9 19.2 %collective-permute-start = (f32[1024,32]{0,1:T(8,128)S(1)}, f32[1024,32]{0,1:T(8,128)S(1)}, u32[]{:S(2)}, u32[]{:S(2)}) collective-permute-start(f32[1024,32]{0,1:T(8,128)S(1)} %bitcast.107), channel_id=1, source_target_pairs={{0,4},{4,8},{8,12},{12,16},{16,20},{20,24},{24,28},{1,5},{5,9},{9,... | collective-permute-start | bytes 393224 | tf_op jit(solution)/shard_map/while/body/eval_jaxpr/ppermute | solution.py:12
  491.8 5.3 copy-start.2
  497.2 1.0 copy-start.1
  537.8 19.1 %collective-permute-start = (f32[1024,32]{0,1:T(8,128)S(1)}, f32[1024,32]{0,1:T(8,128)S(1)}, u32[]{:S(2)}, u32[]{:S(2)}) collective-permute-start(f32[1024,32]{0,1:T(8,128)S(1)} %bitcast.107), channel_id=1, source_target_pairs={{0,4},{4,8},{8,12},{12,16},{16,20},{20,24},{24,28},{1,5},{5,9},{9,... | collective-permute-start | bytes 393224 | tf_op jit(solution)/shard_map/while/body/eval_jaxpr/ppermute | solution.py:12
  551.6 5.3 copy-start.2
  557.0 1.0 copy-start.1
  597.8 19.1 %collective-permute-start = (f32[1024,32]{0,1:T(8,128)S(1)}, f32[1024,32]{0,1:T(8,128)S(1)}, u32[]{:S(2)}, u32[]{:S(2)}) collective-permute-start(f32[1024,32]{0,1:T(8,128)S(1)} %bitcast.107), channel_id=1, source_target_pairs={{0,4},{4,8},{8,12},{12,16},{16,20},{20,24},{24,28},{1,5},{5,9},{9,... | collective-permute-start | bytes 393224 | tf_op jit(solution)/shard_map/while/body/eval_jaxpr/ppermute | solution.py:12
  611.6 5.3 copy-start.2
  616.9 1.0 copy-start.1
  658.0 18.9 %collective-permute-start = (f32[1024,32]{0,1:T(8,128)S(1)}, f32[1024,32]{0,1:T(8,128)S(1)}, u32[]{:S(2)}, u32[]{:S(2)}) collective-permute-start(f32[1024,32]{0,1:T(8,128)S(1)} %bitcast.107), channel_id=1, source_target_pairs={{0,4},{4,8},{8,12},{12,16},{16,20},{20,24},{24,28},{1,5},{5,9},{9,... | collective-permute-start | bytes 393224 | tf_op jit(solution)/shard_map/while/body/eval_jaxpr/ppermute | solution.py:12
  671.5 5.3 copy-start.2
  676.9 5.3 copy-start.15
  676.9 5.3 copy-start.16
  676.9 5.3 copy-start.17
  676.9 5.3 copy-start.18
  682.2 2.2 copy-start
  682.2 2.4 copy-start.13
  682.2 2.4 copy-start.14
  684.2 0.8 copy-start.11
  684.2 0.8 copy-start.12
  684.7 0.7 copy-start.9
  684.7 0.7 copy-start.10
  685.7 7.5 %copy-start.4 = (f32[1,4096]{1,0:T(1,128)S(1)}, f32[1,4096]{1,0:T(1,128)}, u32[]{:S(2)}) copy-start(f32[1,4096]{1,0:T(1,128)} %get-tuple-element.339) | copy-start | bytes 49156
  685.7 7.5 %copy-start.8 = (f32[1,4096]{1,0:T(1,128)S(1)}, f32[1,4096]{1,0:T(1,128)}, u32[]{:S(2)}) copy-start(f32[1,4096]{1,0:T(1,128)} %get-tuple-element.344) | copy-start | bytes 49156
  693.0 0.7 copy-start.7
  693.4 0.7 copy-start.6
  (2 other events, 1.4 us)
where the time goes:
time: 709 us; the launch traced here: 704 us
  blocking collectives  300 us (42%)
  other arithmetic  173 us (24%)
  matrix products  145 us (20%)
  starting transfers between devices  74.1 us (10%)
  local copies, waits for them, and re-layouts  9.94 us (1%)
    all_gather x22, blocking collectives, advance(): full = lax.all_gather(current, 'tile', axis=0, tiled=True)  300 us
    dot_general x22, matrix products, advance(): jnp.dot(interface[layer_num], phased, preferred_element_type=jnp.float32)  131 us
    ppermute x11, starting transfers between devices, shifted(): return lax.ppermute(x, axis, pairs)  74.1 us
    select_n x11, other arithmetic, step_blocks(): jnp.where(valid, put_block(store_full, fulls, clipped, block_width, half)...  57.7 us
    while x22, other arithmetic  50.2 us
    mul x24, other arithmetic, rotate(): cosine = (scale * jnp.cos(frac * angle_row))[:, None]  25.5 us
    dot_general x2, matrix products, on_device(): jnp.dot(eigvec[layer_num], depth, preferred_element_type=jnp.float32)  14.4 us
  transfers between devices with their start and end apart: 11, of which 0 were waited for; matrix products, arithmetic and copies ran while one was open for 19% of the time, Pallas kernels for 0%

commit v1 on v0

v1 whole, which is shorter than its diff:
```python
import functools

import jax
import jax.numpy as jnp
from jax import lax
from jax.experimental import pallas as pl
from jax.experimental.pallas import tpu as pltpu
from jax.sharding import PartitionSpec as P

DEPTHS = 4
WIDTH = 8
MESH = pl.DeviceIdType.MESH
NT = (((1,), (1,)), ((), ()))


def stack_kernel(
    groups, tiles, inc_ref, tab_ref, s_hbm, w_hbm, fields_ref, leave_ref,
    enter, sent, s_v, w_v, total, s_sem, w_sem, inc_send, send, recv,
):
    layers, blocks, width2, rows = sent.shape
    width = width2 // 2
    group = lax.axis_index("layer")
    tile = lax.axis_index("tile")
    toward = 1 - 2 * (tile // ((tiles + 1) // 2))

    def order(k):
        return lax.rem(tile + toward * k + tiles, tiles)

    def load(hbm, vmem, sem, j, t):
        cols = pl.ds(pl.multiple_of(t * rows, rows), rows)
        return pltpu.make_async_copy(hbm.at[j, :, cols], vmem.at[j, t], sem.at[j, t])

    for hbm, vmem, sem in ((s_hbm, s_v, s_sem), (w_hbm, w_v, w_sem)):
        for j in range(layers):
            for k in range(tiles):
                load(hbm, vmem, sem, j, order(k) if hbm is s_hbm else k).start()

    barrier = pltpu.get_barrier_semaphore()
    after = lax.rem(group + 1, groups)
    before = lax.rem(group + groups - 1, groups)
    for k in range(tiles):
        pl.semaphore_signal(barrier, inc=1, device_id=(after, order(k)), device_id_type=MESH)
        pl.semaphore_signal(barrier, inc=1, device_id=(before, order(k)), device_id_type=MESH)
        if k:
            pl.semaphore_signal(barrier, inc=1, device_id=(group, order(k)), device_id_type=MESH)
    pl.semaphore_wait(barrier, 3 * tiles - 1)

    def incident_copy(b, k):
        return pltpu.make_async_remote_copy(
            src_ref=inc_ref.at[b], dst_ref=enter.at[0, b, tile], send_sem=inc_send.at[b, k],
            recv_sem=recv.at[0, b, tile], device_id=(group, order(k)), device_id_type=MESH,
        )

    def leaving_copy(j, b, k):
        last = j == layers - 1
        return pltpu.make_async_remote_copy(
            src_ref=sent.at[j, b], dst_ref=enter.at[0 if last else j + 1, b, tile],
            send_sem=send.at[j, b, k], recv_sem=recv.at[0 if last else j + 1, b, tile],
            device_id=(after if last else group, order(k)), device_id_type=MESH,
        )

    def arrived(j, b, t):
        pltpu.make_async_copy(enter.at[j, b, t], enter.at[j, b, t], recv.at[j, b, t]).wait()

    def send_incident(b):
        for k in range(tiles - 1, 0, -1):
            incident_copy(b, k).start()
        pltpu.make_async_copy(inc_ref.at[b], enter.at[0, b, tile], recv.at[0, b, tile]).start()

    @pl.when(group == 0)
    def _():
        send_incident(0)

    def factors(j, t, step):
        row = 2 * (step - 1)
        return tab_ref[j, t, row : row + 1, :], tab_ref[j, t, row + 1 : row + 2, :]

    def through(j, b):
        def chunk(k, acc):
            t = order(k)

            @pl.when(b == 0)
            def _():
                load(s_hbm, s_v, s_sem, j, t).wait()

            if j == 0:
                arrived(j, b, t)
            else:
                @pl.when(k > 0)
                def _():
                    arrived(j, b, t)

            cosine, sine = factors(j, t, DEPTHS)
            real_part = enter[j, b, t, :width, :]
            imag_part = enter[j, b, t, width:, :]
            phased = jnp.concatenate(
                [cosine * real_part - sine * imag_part, sine * real_part + cosine * imag_part], axis=0
            ).astype(jnp.bfloat16)
            return acc + lax.dot_general(phased, s_v[j, t], NT, preferred_element_type=jnp.float32)

        acc = lax.fori_loop(0, tiles, chunk, jnp.zeros((width2, rows), jnp.float32))
        sent[j, b] = acc
        if j < layers - 1:
            enter[j + 1, b, tile] = acc
            for k in range(tiles - 1, 0, -1):
                leaving_copy(j, b, k).start()
        else:
            @pl.when(group < groups - 1)
            def _():
                for k in range(tiles - 1, -1, -1):
                    leaving_copy(j, b, k).start()

    def recover(j):
        def chunk(t, carry):
            load(w_hbm, w_v, w_sem, j, t).wait()
            real_part = jnp.concatenate([enter[j, b, t, :width, :] for b in range(blocks)], axis=0)
            imag_part = jnp.concatenate([enter[j, b, t, width:, :] for b in range(blocks)], axis=0)
            for step in range(DEPTHS):
                if step == 0:
                    parts = [real_part, imag_part]
                else:
                    cosine, sine = factors(j, t, step)
                    parts = [
                        cosine * real_part - sine * imag_part, sine * real_part + cosine * imag_part
                    ]
                depth = jnp.concatenate(parts, axis=0).astype(jnp.bfloat16)
                piece = lax.dot_general(depth, w_v[j, t], NT, preferred_element_type=jnp.float32)
                total[step] = jnp.where(t == 0, piece, total[step] + piece)
            return carry

        lax.fori_loop(0, tiles, chunk, 0)
        for step in range(DEPTHS):
            cols = 2 * width * blocks
            fields_ref[j, :, step * cols : (step + 1) * cols] = total[step].T.astype(jnp.bfloat16)

    def block_step(b, carry):
        for j in range(layers):
            through(j, b)
            if j == 0:
                @pl.when((group == 0) & (b < blocks - 1))
                def _():
                    send_incident(b + 1)
            if j < layers - 1:
                @pl.when(b == blocks - 1)
                def _():
                    recover(j)
        return carry

    total[...] = jnp.zeros_like(total)
    lax.fori_loop(0, blocks, block_step, 0)
    recover(layers - 1)
    for j in range(layers):
        real_part = jnp.concatenate([sent[j, b, :width, :] for b in range(blocks)], axis=0)
        imag_part = jnp.concatenate([sent[j, b, width:, :] for b in range(blocks)], axis=0)
        leave_ref[j] = jnp.concatenate([real_part, imag_part], axis=0).T

    def drain(b, carry):
        for j in range(layers - 1):
            for k in range(1, tiles):
                leaving_copy(j, b, k).wait_send()

        @pl.when(group < groups - 1)
        def _():
            for k in range(tiles):
                leaving_copy(layers - 1, b, k).wait_send()

        @pl.when(group == 0)
        def _():
            for k in range(1, tiles):
                incident_copy(b, k).wait_send()

        return carry

    lax.fori_loop(0, blocks, drain, 0)


def on_device(incident, interface, eigvec, angle, decay):
    groups = lax.axis_size("layer")
    tiles = lax.axis_size("tile")
    layers, rows, orders = interface.shape
    cols = incident.shape[1]
    blocks = cols // 2 // WIDTH
    amps = incident.astype(jnp.float32).T.reshape(2, blocks, WIDTH, rows)
    amps = amps.transpose(1, 0, 2, 3).reshape(blocks, 2 * WIDTH, rows)
    frac = (jnp.arange(1, DEPTHS + 1, dtype=jnp.float32) / DEPTHS)[None, :, None]
    scale = jnp.exp(-frac * decay[:, None, :])
    cosine = scale * jnp.cos(frac * angle[:, None, :])
    sine = scale * jnp.sin(frac * angle[:, None, :])
    table = jnp.stack([cosine, sine], axis=2).reshape(layers, 2 * DEPTHS, tiles, rows)
    table = table.transpose(0, 2, 1, 3)
    vmem = pl.BlockSpec(memory_space=pltpu.VMEM)
    anywhere = pl.BlockSpec(memory_space=pl.ANY)
    return pl.pallas_call(
        functools.partial(stack_kernel, groups, tiles),
        out_shape=(
            jax.ShapeDtypeStruct((layers, rows, DEPTHS * cols), jnp.bfloat16),
            jax.ShapeDtypeStruct((layers, rows, cols), jnp.float32),
        ),
        in_specs=[vmem, vmem, anywhere, anywhere],
        out_specs=(vmem, vmem),
        scratch_shapes=[
            pltpu.VMEM((layers, blocks, tiles, 2 * WIDTH, rows), jnp.float32),
            pltpu.VMEM((layers, blocks, 2 * WIDTH, rows), jnp.float32),
            pltpu.VMEM((layers, tiles, rows, rows), jnp.bfloat16),
            pltpu.VMEM((layers, tiles, rows, rows), jnp.bfloat16),
            pltpu.VMEM((DEPTHS, cols, rows), jnp.float32),
            pltpu.SemaphoreType.DMA((layers, tiles)),
            pltpu.SemaphoreType.DMA((layers, tiles)),
            pltpu.SemaphoreType.DMA((blocks, tiles)),
            pltpu.SemaphoreType.DMA((layers, blocks, tiles)),
            pltpu.SemaphoreType.DMA((layers, blocks, tiles)),
        ],
        compiler_params=pltpu.CompilerParams(
            collective_id=0, has_side_effects=True, vmem_limit_bytes=60 * 2**20
        ),
        name="stack",
    )(amps, table, interface, eigvec)


def solution(mesh):
    in_specs = (
        P("tile", None),
        P("layer", "tile", None),
        P("layer", "tile", None),
        P("layer", None),
        P("layer", None),
    )
    out_specs = (P("layer", "tile", None), P("layer", "tile", None))
    return jax.shard_map(
        on_device, mesh=mesh, in_specs=in_specs, out_specs=out_specs, check_vma=False
    )
```

time: 709 us -> 303 us (0.43)
  the two profiles are of different devices: /device:TPU:1 before, /device:TPU:15 now
where the time goes in v1:
time: 303 us
  Pallas kernels  292 us (96%)
  local copies, waits for them, and re-layouts  8.56 us (3%)
    pallas_call x1, Pallas kernels, on_device(): pl.pallas_call(functools.partial(stack_kernel, groups, tiles), out_shape=...  292 us
    unnamed x3, local copies, waits for them, and re-layouts  6.39 us

profile of v1, /device:TPU:15, one launch (start us, length us, event | category | flops | bytes accessed | tf_op | source)
XLA Modules:
  0.0 303.0 jit_solution(10152549323756251916)
XLA Ops:
  0.6 1.9 fusion
  2.5 0.1 pad_maximum_fusion
  2.6 0.2 copy.13
  2.8 0.3 reshape.51
  3.1 0.9 copy.18
  4.0 1.1 copy.11
  5.1 0.8 copy.17
  5.9 291.8 %stack.7 = (bf16[2,1024,512]{2,1,0:T(8,128)(2,1)}, f32[2,1024,128]{2,1,0:T(8,128)}) custom-call(f32[8,16,1024]{2,1,0:T(8,128)} %bitcast.11, f32[2,4,8,1024]{3,2,1,0:T(8,128)} %bitcast.13, bf16[2,1024,4096]{2,1,0:T(8,128)(2,1)} %s_hbm.1, bf16[2,1024,4096]{2,1,0:T(8,128)(2,1)} %w_hbm.1), custom_call_target="tpu_custom_call" | custom-call | tf_op jit(solution)/shard_map/stack/pallas_call | solution.py:193
  297.7 3.0 %copy.21 = bf16[2,1024,512]{2,1,0:T(8,128)(2,1)} copy(bf16[2,1024,512]{2,1,0:T(8,128)(2,1)} %get-tuple-element.8) | data formatting | bytes 4194304
  300.7 2.3 copy.22
  (2 shorter events, 0.1 us)

commit v2 on v1

--- a/solution.py
+++ b/solution.py
@@ -8,20 +8,26 @@
 from jax.sharding import PartitionSpec as P
 
 DEPTHS = 4
-WIDTH = 8
+WIDTH = 16
+RELAY = True
 MESH = pl.DeviceIdType.MESH
 NT = (((1,), (1,)), ((), ()))
 
 
 def stack_kernel(
     groups, tiles, inc_ref, tab_ref, s_hbm, w_hbm, fields_ref, leave_ref,
-    enter, sent, s_v, w_v, total, s_sem, w_sem, inc_send, send, recv,
+    enter, sent, s_v, w_v, total, s_sem, w_sem, inc_send, send, recv, pass_send,
 ):
     layers, blocks, width2, rows = sent.shape
     width = width2 // 2
     group = lax.axis_index("layer")
     tile = lax.axis_index("tile")
     toward = 1 - 2 * (tile // ((tiles + 1) // 2))
+
+    end = (tile == 0) | (tile == tiles - 1)
+    relays = RELAY and tiles > 3
+    relay = (tile == 1) | (tile == tiles - 2)
+    far = jnp.where(tile == 1, tiles - 1, 0)
 
     def order(k):
         return lax.rem(tile + toward * k + tiles, tiles)
@@ -62,14 +68,29 @@
     def arrived(j, b, t):
         pltpu.make_async_copy(enter.at[j, b, t], enter.at[j, b, t], recv.at[j, b, t]).wait()
 
+    def passed_copy(j, b):
+        return pltpu.make_async_remote_copy(
+            src_ref=enter.at[j, b, far], dst_ref=enter.at[j, b, far], send_sem=pass_send.at[j, b],
+            recv_sem=recv.at[j, b, far], device_id=(group, tiles - 1 - far), device_id_type=MESH,
+        )
+
+    def each_target(first, act):
+        for k in range(tiles - 1, first - 1, -1):
+            if relays and k == tiles - 1:
+                @pl.when(jnp.logical_not(end))
+                def _():
+                    act(k)
+            else:
+                act(k)
+
     def send_incident(b):
-        for k in range(tiles - 1, 0, -1):
-            incident_copy(b, k).start()
+        each_target(1, lambda k: incident_copy(b, k).start())
         pltpu.make_async_copy(inc_ref.at[b], enter.at[0, b, tile], recv.at[0, b, tile]).start()
 
     @pl.when(group == 0)
     def _():
-        send_incident(0)
+        for b in range(1):
+            send_incident(b)
 
     def factors(j, t, step):
         row = 2 * (step - 1)
@@ -89,6 +110,11 @@
                 @pl.when(k > 0)
                 def _():
                     arrived(j, b, t)
+
+            if relays:
+                @pl.when(relay & (t == far))
+                def _():
+                    passed_copy(j, b).start()
 
             cosine, sine = factors(j, t, DEPTHS)
             real_part = enter[j, b, t, :width, :]
@@ -102,13 +128,11 @@
         sent[j, b] = acc
         if j < layers - 1:
             enter[j + 1, b, tile] = acc
-            for k in range(tiles - 1, 0, -1):
-                leaving_copy(j, b, k).start()
+            each_target(1, lambda k: leaving_copy(j, b, k).start())
         else:
             @pl.when(group < groups - 1)
             def _():
-                for k in range(tiles - 1, -1, -1):
-                    leaving_copy(j, b, k).start()
+                each_target(0, lambda k: leaving_copy(j, b, k).start())
 
     def recover(j):
         def chunk(t, carry):
@@ -144,6 +168,7 @@
                 @pl.when(b == blocks - 1)
                 def _():
                     recover(j)
+
         return carry
 
     total[...] = jnp.zeros_like(total)
@@ -156,18 +181,21 @@
 
     def drain(b, carry):
         for j in range(layers - 1):
-            for k in range(1, tiles):
-                leaving_copy(j, b, k).wait_send()
+            each_target(1, lambda k: leaving_copy(j, b, k).wait_send())
 
         @pl.when(group < groups - 1)
         def _():
-            for k in range(tiles):
-                leaving_copy(layers - 1, b, k).wait_send()
+            each_target(0, lambda k: leaving_copy(layers - 1, b, k).wait_send())
 
         @pl.when(group == 0)
         def _():
-            for k in range(1, tiles):
-                incident_copy(b, k).wait_send()
+            each_target(1, lambda k: incident_copy(b, k).wait_send())
+
+        if relays:
+            @pl.when(relay)
+            def _():
+                for j in range(layers):
+                    passed_copy(j, b).wait_send()
 
         return carry
 
@@ -209,6 +237,7 @@
             pltpu.SemaphoreType.DMA((blocks, tiles)),
             pltpu.SemaphoreType.DMA((layers, blocks, tiles)),
             pltpu.SemaphoreType.DMA((layers, blocks, tiles)),
+            pltpu.SemaphoreType.DMA((layers, blocks)),
         ],
         compiler_params=pltpu.CompilerParams(
             collective_id=0, has_side_effects=True, vmem_limit_bytes=60 * 2**20

time: 303 us -> 286 us (0.944); the launches traced: 303 us -> 283 us
  Pallas kernels: 292 us -> 271 us
    pallas_call x1, Pallas kernels: 292 us -> 271 us  [on_device(): pl.pallas_call(functools.partial(stack_kernel, groups, tiles), out_shape=...]
where the time goes in v2:
time: 286 us; the launch traced here: 283 us
  Pallas kernels  271 us (95%)
  local copies, waits for them, and re-layouts  8.56 us (3%)
    pallas_call x1, Pallas kernels, on_device(): pl.pallas_call(functools.partial(stack_kernel, groups, tiles), out_shape=...  271 us
    unnamed x3, local copies, waits for them, and re-layouts  6.39 us

profile of v2, /device:TPU:15, one launch (start us, length us, event | category | flops | bytes accessed | tf_op | source)
XLA Modules:
  0.0 282.6 jit_solution(5336714362259860882)
XLA Ops:
  0.6 1.9 fusion
  2.5 0.1 pad_maximum_fusion
  2.6 0.2 copy.13
  2.8 0.3 reshape.51
  3.1 0.9 copy.16
  4.0 1.1 copy.11
  5.1 0.8 copy.12
  5.9 271.4 %stack.7 = (bf16[2,1024,512]{2,1,0:T(8,128)(2,1)}, f32[2,1024,128]{2,1,0:T(8,128)}) custom-call(f32[4,32,1024]{2,1,0:T(8,128)} %bitcast.9, f32[2,4,8,1024]{3,2,1,0:T(8,128)} %bitcast.11, bf16[2,1024,4096]{2,1,0:T(8,128)(2,1)} %s_hbm.1, bf16[2,1024,4096]{2,1,0:T(8,128)(2,1)} %w_hbm.1), custom_call_target="tpu_custom_call" | custom-call | tf_op jit(solution)/shard_map/stack/pallas_call | solution.py:221
  277.3 3.0 %copy.19 = bf16[2,1024,512]{2,1,0:T(8,128)(2,1)} copy(bf16[2,1024,512]{2,1,0:T(8,128)(2,1)} %get-tuple-element.8) | data formatting | bytes 4194304
  280.4 2.3 copy.20
  (2 shorter events, 0.1 us)
